TPU v7x, 256 devices: a whole 4x4x8 slice. The times are simulated.
256 devices in a mesh: pair: 64 (over y, z, core), aux: 4 (over x).
Axes of the slice: x: 4, y: 4, z: 8, core: 2. Of those that a mesh axis runs over, the one named last changes fastest.
Arguments:
- factors: bfloat16 [64, 8192, 8, 128], P('pair', 'aux'), may hold values from -0.0625 to 0.0625
- amplitudes: bfloat16 [3072, 128, 128], P('pair'), may hold values from -6 to 6
- block_list: int32 [3072, 3], P('pair'), may hold values from 0 to 63, as said below
- owner_map: int32 [64], replicated, may hold values from 0 to 63, as said below
Outputs:
- residual_blocks: bfloat16 [3072, 128, 128], P('pair')
Inputs may be any that keep to these rules, and one draw needn't show every extreme that they name: `block_list`: each row (k, A, C) names an occupied orbital below 64 and two virtual blocks below 8; no row repeats. Among the 48 rows of one device at most 2 have orbitals with the same owner_map entry, and exactly 2 for some entry on every device. `owner_map`: A permutation: entry k is the row of factors that holds orbital k.
All inputs are finite; a program needn't handle non-finite values.
Results may differ from a plain program's by a relative error of at most 0.0046.
Values may be sent and summed in bfloat16 or wider, within the bound.
A program may use at most 64 MiB of HBM per device.

v0:
```python
import jax
import jax.numpy as jnp
from jax import lax
from jax.sharding import PartitionSpec as P

CAP = 2


def on_device(factors, amplitudes, block_list, owner_map):
    pair_count = lax.axis_size("pair")
    slot_total = pair_count * CAP
    block_count = amplitudes.shape[0]
    block_width = amplitudes.shape[1]
    virt_blocks = factors.shape[2]
    share_rows = factors.shape[1]
    orbital_total = owner_map.shape[0]
    orbitals = block_list[:, 0]
    block_a = block_list[:, 1]
    block_c = block_list[:, 2]
    matches = orbitals[:, None] == lax.iota(jnp.int32, orbital_total)[None, :]
    owners = jnp.sum(jnp.where(matches, owner_map[None, :], 0), axis=1)
    owner_hits = (owners[:, None] == lax.iota(jnp.int32, pair_count)[None, :]).astype(jnp.int32)
    earlier = jnp.cumsum(owner_hits, axis=0) - owner_hits
    slot_rank = jnp.sum(earlier * owner_hits, axis=1)
    slots = owners * CAP + slot_rank
    placing = slots[:, None] == lax.iota(jnp.int32, slot_total)[None, :]
    place_matrix = placing.astype(jnp.bfloat16)
    flat_blocks = amplitudes.reshape(block_count, block_width * block_width)
    send_blocks = jnp.einsum(
        "js,jm->sm", place_matrix, flat_blocks, preferred_element_type=jnp.float32
    )
    send_blocks = send_blocks.astype(jnp.bfloat16).reshape(
        pair_count, CAP, block_width, block_width
    )
    send_a = jnp.sum(jnp.where(placing, block_a[:, None] + 1, 0), axis=0)
    send_c = jnp.sum(jnp.where(placing, block_c[:, None] + 1, 0), axis=0)
    send_index = (
        jnp.stack([send_a, send_c], axis=-1).astype(jnp.bfloat16).reshape(pair_count, CAP, 2)
    )
    recv_blocks, recv_index = (
        lax.all_to_all(send_blocks, "pair", split_axis=0, concat_axis=0, tiled=True),
        lax.all_to_all(send_index, "pair", split_axis=0, concat_axis=0, tiled=True),
    )
    recv_index = recv_index.reshape(slot_total, 2).astype(jnp.int32) - 1
    slot_a = recv_index[:, 0]
    slot_c = recv_index[:, 1]
    onehot_a = (slot_a[:, None] == lax.iota(jnp.int32, virt_blocks)[None, :]).astype(jnp.bfloat16)
    onehot_c = (slot_c[:, None] == lax.iota(jnp.int32, virt_blocks)[None, :]).astype(jnp.bfloat16)
    combined = (onehot_c[:, :, None] * onehot_a[:, None, :]).reshape(
        slot_total, virt_blocks * virt_blocks
    )
    recv_flat = recv_blocks.reshape(slot_total, block_width * block_width)
    weights = jnp.einsum("sm,sn->mn", combined, recv_flat, preferred_element_type=jnp.float32)
    weights = weights.reshape(virt_blocks, virt_blocks, block_width, block_width)
    weights = jnp.transpose(weights, (0, 3, 1, 2)).reshape(
        virt_blocks * block_width, virt_blocks * block_width
    )
    weights = weights.astype(jnp.bfloat16)
    factor_flat = factors.reshape(share_rows, virt_blocks * block_width)
    factor_rows = factor_flat
    inter_share = lax.psum_scatter(
        jnp.dot(factor_rows, weights, preferred_element_type=jnp.float32),
        "pair",
        scatter_dimension=0,
        tiled=True,
    )
    inter_share = inter_share.astype(jnp.bfloat16)
    shard_rows = lax.all_gather(inter_share, "pair", axis=0, tiled=True)
    height = shard_rows.shape[0]
    factor_rows = factor_flat
    left = shard_rows.reshape(height, virt_blocks, block_width)
    right = factor_rows.reshape(height, virt_blocks, block_width)
    projected = jnp.einsum("qAa,qCc->ACac", left, right, preferred_element_type=jnp.float32)
    safe_a = jnp.maximum(slot_a, 0)
    safe_c = jnp.maximum(slot_c, 0)
    summed = lax.psum(projected, "aux")
    picked = summed[safe_a, safe_c].astype(jnp.bfloat16)
    picked = picked.reshape(pair_count, CAP, block_width, block_width)
    returned = lax.all_to_all(picked, "pair", split_axis=0, concat_axis=0, tiled=True)
    returned = returned.reshape(slot_total, block_width * block_width)
    result = jnp.einsum("js,sm->jm", place_matrix, returned, preferred_element_type=jnp.float32)
    return result.astype(jnp.bfloat16).reshape(block_count, block_width, block_width)


def solution(mesh):
    placed = (P("pair", "aux", None, None), P("pair", None, None), P("pair", None), P())
    return jax.shard_map(
        on_device, mesh=mesh, in_specs=placed, out_specs=P("pair", None, None), check_vma=False
    )
```

profile of v0, /device:TPU:1, one launch (start us, length us, event | category | flops | bytes accessed | tf_op | source)
XLA Modules:
  0.0 617.8 jit_solution(2545537378293932037)
XLA Ops:
  6.5 0.8 add_bitcast_fusion
  7.3 0.8 select_reduce_fusion.3
  8.3 0.2 select_reduce_fusion.2
  8.7 0.1 stack.10
  8.8 0.2 stack.9
  9.0 0.7 copy.26
  9.6 13.2 %all-to-all-start = ((bf16[64,2,2]{1,2,0:T(2,128)(2,1)}), bf16[64,2,2]{1,2,0:T(2,128)(2,1)S(1)}, u32[]{:S(2)}, u32[]{:S(2)}) async-start(bf16[64,2,2]{1,2,0:T(2,128)(2,1)} %copy.26), calls=%async_computation | async-start | bytes 65536 | tf_op jit(solution)/shard_map/all_to_all | solution.py:42
  22.8 2.8 fusion.10
  25.6 3.2 copy.39
  28.8 3.2 all-to-all-done
  32.0 7.3 %all-to-all-start.1 = ((bf16[64,2,128,128]{3,2,1,0:T(8,128)(2,1)}), bf16[64,2,128,128]{3,2,1,0:T(8,128)(2,1)}, u32[]{:S(2)}, u32[]{:S(2)}) async-start(bf16[64,2,128,128]{3,2,1,0:T(8,128)(2,1)} %bitcast.84), calls=%async_computation.1 | async-start | bytes 8388608 | tf_op jit(solution)/shard_map/all_to_all | solution.py:41
  39.3 0.2 reduce-scatter.4.cloned.1.call-start
  39.7 0.1 copy.28
  39.8 0.1 sub.11
  40.0 95.3 %all-to-all-done.1 = bf16[64,2,128,128]{3,2,1,0:T(8,128)(2,1)} async-done(((bf16[64,2,128,128]{3,2,1,0:T(8,128)(2,1)}), bf16[64,2,128,128]{3,2,1,0:T(8,128)(2,1)}, u32[]{:S(2)}, u32[]{:S(2)}) %all-to-all-start.1) | async-done | bytes 4194336 | tf_op jit(solution)/shard_map/all_to_all | solution.py:41
  135.2 7.7 %copy.70 = bf16[16,8,128,128]{3,1,2,0:T(8,128)(2,1)} copy(bf16[16,8,128,128]{3,2,1,0:T(8,128)(2,1)} %bitcast.39) | data formatting | bytes 8388608
  142.9 6.4 %copy.29 = bf16[128,16384]{0,1:T(8,128)(2,1)} copy(bf16[128,16384]{1,0:T(8,128)(2,1)} %bitcast.88) | data formatting | bytes 8388608 | tf_op jit(solution)/shard_map/reshape | solution.py:52
  149.3 3.8 convert_bitcast_fusion
  153.1 3.3 copy.30
  156.3 10.6 %convolution_bitcast_fusion = f32[2048,1024]{0,1:T(8,128)} fusion(bf16[256,8,8,128]{3,2,1,0:T(8,128)(2,1)} %bitcast.92, bf16[128,8,8,128]{3,2,1,0:T(8,128)(2,1)} %bitcast.90), kind=kOutput, calls=%fused_computation.3 | convolution fusion | flops 4294967296 | bytes 14680064 | tf_op jit(solution)/shard_map/dot_general | solution.py:62
  166.9 9.3 %copy.36 = f32[2048,1024]{1,0:T(8,128)} copy(f32[2048,1024]{0,1:T(8,128)} %convolution_bitcast_fusion) | data formatting | bytes 16777216
  176.2 0.3 all-gather.2.cloned.1.call-start
  176.5 143.6 %reduce-scatter.4.cloned.1.call-done = f32[32,1024]{1,0:T(8,128)} async-done(((f32[2048,1024]{1,0:T(8,128)}), f32[32,1024]{1,0:T(8,128)}) %reduce-scatter.4.cloned.1.call-update) | async-done | bytes 131088 | tf_op jit(solution)/shard_map/reduce_scatter | solution.py:61
  320.2 1.5 convert_element_type.57
  321.7 83.6 %all-gather.2.cloned.1.call-done = bf16[2048,1024]{1,0:T(8,128)(2,1)} async-done(((bf16[32,1024]{1,0:T(8,128)(2,1)}), bf16[2048,1024]{1,0:T(8,128)(2,1)}) %all-gather.2.cloned.1.call-update) | async-done | bytes 4194320 | tf_op jit(solution)/shard_map/all_gather | solution.py:68
  405.3 6.5 %copy.32 = bf16[2048,1024]{0,1:T(8,128)(2,1)} copy(bf16[2048,1024]{1,0:T(8,128)(2,1)} %all-gather.2.cloned.1.call-done) | data formatting | bytes 8388608 | tf_op jit(solution)/shard_map/all_gather | solution.py:68
  411.8 9.9 %fusion.7 = f32[8,8,128,128]{3,2,1,0:T(8,128)} fusion(bf16[2048,8,128,1]{0,2,3,1:T(8,128)(2,1)} %bitcast.89, bf16[2048,8,128]{2,1,0:T(8,128)(2,1)} %bitcast.93), kind=kOutput, calls=%fused_computation.12 | convolution fusion | flops 4294967296 | bytes 12582912 | tf_op jit(solution)/shard_map/qAa,qCc->ACac/dot_general | solution.py:73
  421.7 78.1 %all-reduce.1 = bf16[8,8,128,128]{3,2,1,0:T(8,128)(2,1)S(1)} all-reduce(f32[8,8,128,128]{3,2,1,0:T(8,128)} %fusion.7), channel_id=1, replica_groups=mesh['pair'=64,'aux'=4] {'aux'}, use_global_device_ids=true, to_apply=%region_6.7 | all-reduce | flops 1048576 | bytes 6291456 | tf_op jit(solution)/shard_map/psum | solution.py:76
  499.8 3.1 gather_fusion
  502.8 103.9 %all_to_all.15 = bf16[64,2,128,128]{3,2,1,0:T(8,128)(2,1)S(1)} all-to-all(bf16[64,2,128,128]{3,2,1,0:T(8,128)(2,1)} %bitcast.86), channel_id=1, replica_groups=mesh['pair'=64,'aux'=4] {'pair'}, dimensions={0} | all-to-all | bytes 8388608 | tf_op jit(solution)/shard_map/all_to_all | solution.py:79
  606.7 2.7 fusion.15
  609.4 1.6 copy.44
  (13 shorter events, 0.4 us)
Async XLA Ops:
  9.6 22.4 %all-to-all-start = ((bf16[64,2,2]{1,2,0:T(2,128)(2,1)}), bf16[64,2,2]{1,2,0:T(2,128)(2,1)S(1)}, u32[]{:S(2)}, u32[]{:S(2)}) async-start(bf16[64,2,2]{1,2,0:T(2,128)(2,1)} %copy.26), calls=%async_computation | async-start | bytes 65536 | tf_op jit(solution)/shard_map/all_to_all | solution.py:42
  32.0 103.2 %all-to-all-start.1 = ((bf16[64,2,128,128]{3,2,1,0:T(8,128)(2,1)}), bf16[64,2,128,128]{3,2,1,0:T(8,128)(2,1)}, u32[]{:S(2)}, u32[]{:S(2)}) async-start(bf16[64,2,128,128]{3,2,1,0:T(8,128)(2,1)} %bitcast.84), calls=%async_computation.1 | async-start | bytes 8388608 | tf_op jit(solution)/shard_map/all_to_all | solution.py:41
  39.3 280.8 %reduce-scatter.4.cloned.1.call-start = ((), (), s32[]{:S(2)}) async-start(), calls=%async_computation.5 | async-start | bytes 8519680 | tf_op jit(solution)/shard_map/reduce_scatter | solution.py:61
  176.2 229.1 %all-gather.2.cloned.1.call-start = ((), (), s32[]{:S(2)}) async-start(), calls=%async_computation.4 | async-start | bytes 4259840 | tf_op jit(solution)/shard_map/all_gather | solution.py:68
Sparse Core Ops, SparseCore 0:
  176.4 143.7 reduce-scatter.3
  323.3 81.9 all-gather.1
where the time goes:
time: 619 us; the launch traced here: 618 us
  waiting for transfers between devices  326 us (53%)
  blocking collectives  182 us (29%)
  local copies, waits for them, and re-layouts  42.2 us (7%)
  matrix products  29.8 us (5%)
  starting transfers between devices  21 us (3%)
  between operations  13.5 us (2%)
    reduce_scatter x1, waiting for transfers between devices, on_device(): lax.psum_scatter(jnp.dot(factor_rows, weights, preferred_element_type=jnp...  144 us
    all_to_all x1, blocking collectives, on_device(): lax.all_to_all(picked, 'pair', split_axis=0, concat_axis=0, tiled=True)  104 us
    all_to_all x1, waiting for transfers between devices, on_device(): lax.all_to_all(send_blocks, 'pair', split_axis=0, concat_axis=0, tiled=True)  95.3 us
    all_gather x1, waiting for transfers between devices, on_device(): shard_rows = lax.all_gather(inter_share, 'pair', axis=0, tiled=True)  83.6 us
    psum x1, blocking collectives, on_device(): summed = lax.psum(projected, 'aux')  78.1 us
    unnamed x4, local copies, waits for them, and re-layouts  21.7 us
    all_to_all x1, starting transfers between devices, on_device(): lax.all_to_all(send_index, 'pair', split_axis=0, concat_axis=0, tiled=True)  13.2 us
  transfers between devices with their start and end apart: 4, of which 4 were waited for; matrix products, arithmetic and copies ran while one was open for 1% of the time, Pallas kernels for 0%

commit v1 on v0

--- a/solution.py
+++ b/solution.py
@@ -73,7 +73,7 @@
     projected = jnp.einsum("qAa,qCc->ACac", left, right, preferred_element_type=jnp.float32)
     safe_a = jnp.maximum(slot_a, 0)
     safe_c = jnp.maximum(slot_c, 0)
-    summed = lax.psum(projected, "aux")
+    summed = jnp.sum(lax.all_gather(projected, "aux"), axis=0)
     picked = summed[safe_a, safe_c].astype(jnp.bfloat16)
     picked = picked.reshape(pair_count, CAP, block_width, block_width)
     returned = lax.all_to_all(picked, "pair", split_axis=0, concat_axis=0, tiled=True)

time: 619 us -> 705 us (1.14)
  waiting for transfers between devices: 326 us -> 479 us
  blocking collectives: 182 us -> 107 us
  other arithmetic: 3.67 us -> 11.9 us
    all_gather x0 -> x1, waiting for transfers between devices: none -> 154 us  [on_device(): summed = jnp.sum(lax.all_gather(projected, 'aux'), axis=0)]
    psum x1 -> x0, blocking collectives: 78.1 us -> none  [on_device(): summed = lax.psum(projected, 'aux')]
    reduce_sum x0 -> x1, other arithmetic: none -> 8.19 us  [on_device(): summed = jnp.sum(lax.all_gather(projected, 'aux'), axis=0)]
  transfers between devices with their start and end apart: 4 -> 5, of which waited for: 4 -> 5; matrix products, arithmetic and copies ran while one was open for 1% -> 1% of each run, Pallas kernels for 0% -> 0%
where the time goes in v1:
time: 705 us; the launch traced here: 704 us
  waiting for transfers between devices  479 us (68%)
  blocking collectives  107 us (15%)
  local copies, waits for them, and re-layouts  42.2 us (6%)
  matrix products  29.7 us (4%)
  starting transfers between devices  21 us (3%)
  between operations  13.2 us (2%)
  other arithmetic  11.9 us (2%)
    all_gather x1, waiting for transfers between devices, on_device(): summed = jnp.sum(lax.all_gather(projected, 'aux'), axis=0)  154 us
    reduce_scatter x1, waiting for transfers between devices, on_device(): lax.psum_scatter(jnp.dot(factor_rows, weights, preferred_element_type=jnp...  144 us
    all_to_all x1, blocking collectives, on_device(): lax.all_to_all(picked, 'pair', split_axis=0, concat_axis=0, tiled=True)  107 us
    all_to_all x1, waiting for transfers between devices, on_device(): lax.all_to_all(send_blocks, 'pair', split_axis=0, concat_axis=0, tiled=True)  95.3 us
    all_gather x1, waiting for transfers between devices, on_device(): shard_rows = lax.all_gather(inter_share, 'pair', axis=0, tiled=True)  83.3 us
    unnamed x4, local copies, waits for them, and re-layouts  21.7 us
  transfers between devices with their start and end apart: 5, of which 5 were waited for; matrix products, arithmetic and copies ran while one was open for 1% of the time, Pallas kernels for 0%

profile of v1, /device:TPU:1, one launch (start us, length us, event | category | flops | bytes accessed | tf_op | source)
XLA Modules:
  0.0 704.3 jit_solution(2927502939980917065)
XLA Ops:
  6.5 0.8 add_bitcast_fusion
  7.3 0.8 select_reduce_fusion.3
  8.3 0.2 select_reduce_fusion.2
  8.7 0.1 stack.10
  8.8 0.2 stack.9
  9.0 0.7 copy.26
  9.6 13.2 %all-to-all-start = ((bf16[64,2,2]{1,2,0:T(2,128)(2,1)}), bf16[64,2,2]{1,2,0:T(2,128)(2,1)S(1)}, u32[]{:S(2)}, u32[]{:S(2)}) async-start(bf16[64,2,2]{1,2,0:T(2,128)(2,1)} %copy.26), calls=%async_computation | async-start | bytes 65536 | tf_op jit(solution)/shard_map/all_to_all | solution.py:42
  22.8 2.8 fusion.10
  25.6 3.2 copy.39
  28.8 3.2 all-to-all-done
  32.0 7.3 %all-to-all-start.1 = ((bf16[64,2,128,128]{3,2,1,0:T(8,128)(2,1)}), bf16[64,2,128,128]{3,2,1,0:T(8,128)(2,1)}, u32[]{:S(2)}, u32[]{:S(2)}) async-start(bf16[64,2,128,128]{3,2,1,0:T(8,128)(2,1)} %bitcast.86), calls=%async_computation.1 | async-start | bytes 8388608 | tf_op jit(solution)/shard_map/all_to_all | solution.py:41
  39.3 0.2 reduce-scatter.4.cloned.1.call-start
  39.8 0.1 sub.11
  40.0 95.3 %all-to-all-done.1 = bf16[64,2,128,128]{3,2,1,0:T(8,128)(2,1)} async-done(((bf16[64,2,128,128]{3,2,1,0:T(8,128)(2,1)}), bf16[64,2,128,128]{3,2,1,0:T(8,128)(2,1)}, u32[]{:S(2)}, u32[]{:S(2)}) %all-to-all-start.1) | async-done | bytes 4194336 | tf_op jit(solution)/shard_map/all_to_all | solution.py:41
  135.2 7.7 %copy.70 = bf16[16,8,128,128]{3,1,2,0:T(8,128)(2,1)} copy(bf16[16,8,128,128]{3,2,1,0:T(8,128)(2,1)} %bitcast.40) | data formatting | bytes 8388608
  142.9 6.4 copy.29
  149.3 3.8 convert_bitcast_fusion
  153.1 3.3 copy.30
  156.3 10.6 %convolution_bitcast_fusion = f32[2048,1024]{0,1:T(8,128)} fusion(bf16[256,8,8,128]{3,2,1,0:T(8,128)(2,1)} %bitcast.94, bf16[128,8,8,128]{3,2,1,0:T(8,128)(2,1)} %bitcast.92), kind=kOutput, calls=%fused_computation.3 | convolution fusion | flops 4294967296 | bytes 14680064 | tf_op jit(solution)/shard_map/dot_general | solution.py:62
  166.9 9.3 %copy.36 = f32[2048,1024]{1,0:T(8,128)} copy(f32[2048,1024]{0,1:T(8,128)} %convolution_bitcast_fusion) | data formatting | bytes 16777216
  176.3 143.9 %reduce-scatter.4.cloned.1.call-done = f32[32,1024]{1,0:T(8,128)} async-done(((f32[2048,1024]{1,0:T(8,128)}), f32[32,1024]{1,0:T(8,128)}) %reduce-scatter.4.cloned.1.call-update) | async-done | bytes 131088 | tf_op jit(solution)/shard_map/reduce_scatter | solution.py:61
  320.2 1.5 convert_element_type.57
  321.7 0.3 all-gather.6.cloned.1.call-start
  322.0 83.3 %all-gather.4.cloned.1.call-done = bf16[2048,1024]{1,0:T(8,128)(2,1)} async-done(((bf16[32,1024]{1,0:T(8,128)(2,1)}), bf16[2048,1024]{1,0:T(8,128)(2,1)}) %all-gather.4.cloned.1.call-update) | async-done | bytes 4194320 | tf_op jit(solution)/shard_map/all_gather | solution.py:68
  405.3 6.5 copy.32
  411.8 9.9 %fusion.7 = f32[8,8,128,128]{3,2,1,0:T(8,128)} fusion(bf16[2048,8,128,1]{0,2,3,1:T(8,128)(2,1)} %bitcast.91, bf16[2048,8,128]{2,1,0:T(8,128)(2,1)} %bitcast.95), kind=kOutput, calls=%fused_computation.12 | convolution fusion | flops 4294967296 | bytes 12582912 | tf_op jit(solution)/shard_map/qAa,qCc->ACac/dot_general | solution.py:73
  421.7 153.6 %all-gather.6.cloned.1.call-done = f32[32,8,128,128]{3,2,1,0:T(8,128)} async-done(((f32[8,8,128,128]{3,2,1,0:T(8,128)}), f32[32,8,128,128]{3,2,1,0:T(8,128)}) %all-gather.6.cloned.1.call-update) | async-done | bytes 16777232 | tf_op jit(solution)/shard_map/all_gather | solution.py:76
  575.4 8.2 %reduce_sum.49 = bf16[8,8,128,128]{3,2,1,0:T(8,128)(2,1)S(1)} reduce(f32[4,8,8,128,128]{4,3,2,1,0:T(8,128)} %bitcast.85, f32[]{:T(128)} %constant.18.clone.1), dimensions={0}, to_apply=%region_6.7 | reduce | flops 3145728 | bytes 18874372 | tf_op jit(solution)/shard_map/reduce_sum | solution.py:76
  583.6 3.1 gather_fusion
  586.6 106.9 %all_to_all.15 = bf16[64,2,128,128]{3,2,1,0:T(8,128)(2,1)S(1)} all-to-all(bf16[64,2,128,128]{3,2,1,0:T(8,128)(2,1)} %bitcast.88), channel_id=1, replica_groups=mesh['pair'=64,'aux'=4] {'pair'}, dimensions={0} | all-to-all | bytes 8388608 | tf_op jit(solution)/shard_map/all_to_all | solution.py:79
  693.5 2.7 fusion.15
  696.2 1.6 copy.44
  (16 shorter events, 0.6 us)
Async XLA Ops:
  9.6 22.4 %all-to-all-start = ((bf16[64,2,2]{1,2,0:T(2,128)(2,1)}), bf16[64,2,2]{1,2,0:T(2,128)(2,1)S(1)}, u32[]{:S(2)}, u32[]{:S(2)}) async-start(bf16[64,2,2]{1,2,0:T(2,128)(2,1)} %copy.26), calls=%async_computation | async-start | bytes 65536 | tf_op jit(solution)/shard_map/all_to_all | solution.py:42
  32.0 103.2 %all-to-all-start.1 = ((bf16[64,2,128,128]{3,2,1,0:T(8,128)(2,1)}), bf16[64,2,128,128]{3,2,1,0:T(8,128)(2,1)}, u32[]{:S(2)}, u32[]{:S(2)}) async-start(bf16[64,2,128,128]{3,2,1,0:T(8,128)(2,1)} %bitcast.86), calls=%async_computation.1 | async-start | bytes 8388608 | tf_op jit(solution)/shard_map/all_to_all | solution.py:41
  39.3 280.8 %reduce-scatter.4.cloned.1.call-start = ((), (), s32[]{:S(2)}) async-start(), calls=%async_computation.6 | async-start | bytes 8519680 | tf_op jit(solution)/shard_map/reduce_scatter | solution.py:61
  176.2 229.1 %all-gather.4.cloned.1.call-start = ((), (), s32[]{:S(2)}) async-start(), calls=%async_computation.4 | async-start | bytes 4259840 | tf_op jit(solution)/shard_map/all_gather | solution.py:68
  321.7 253.6 %all-gather.6.cloned.1.call-start = ((), (), s32[]{:S(2)}) async-start(), calls=%async_computation.5 | async-start | bytes 20971520 | tf_op jit(solution)/shard_map/all_gather | solution.py:76
Sparse Core Ops, SparseCore 0:
  176.4 143.7 reduce-scatter.3
  323.3 81.9 all-gather.3
  421.8 153.4 all-gather.5
